TPU v7x, 32 devices: a whole 2x2x4 slice. The times are simulated.
32 devices in a mesh: ctx: 16 (over z, y, x), head: 2 (over core).
Axes of the slice: x: 2, y: 2, z: 4, core: 2. Of those that a mesh axis runs over, the one named last changes fastest.
Arguments:
- queries: bfloat16 [8192, 4, 4, 128], P('ctx', 'head')
- keys: bfloat16 [8192, 4, 128], P('ctx')
- values: bfloat16 [8192, 4, 128], P('ctx'), may hold values from -6 to 6
- output_gradient: bfloat16 [8192, 4, 4, 128], P('ctx', 'head'), may hold values from -6 to 6
- selected: int32 [16, 2], replicated, may hold values from 0 to 14, as said below
Outputs:
- attn_out: bfloat16 [8192, 4, 4, 128], P('ctx', 'head')
- grad_q: bfloat16 [8192, 4, 4, 128], P('ctx', 'head')
- grad_k: bfloat16 [8192, 4, 128], P('ctx', 'head')
- grad_v: bfloat16 [8192, 4, 128], P('ctx', 'head')
Inputs may be any that keep to these rules, and one draw needn't show every extreme that they name: selected[b, j] <= b for every block b; an entry equal to b selects no block; for b >= 2 the two entries of a row differ and both are below b.
All inputs are finite; a program needn't handle non-finite values.
Results may differ from a plain program's by a relative error of at most 0.011.
Values may be sent and summed in bfloat16 or wider, within the bound.
A program may use at most 128 MiB of HBM per device.

v0:
```python
import jax
import jax.numpy as jnp
from jax import lax
from jax.sharding import PartitionSpec as P


def fetch_blocks(own_keys, own_values, selected, piece_rows):
    held_keys, held_values = (
        lax.all_to_all(own_keys, "ctx", split_axis=0, concat_axis=0, tiled=True),
        lax.all_to_all(own_values, "ctx", split_axis=0, concat_axis=0, tiled=True),
    )
    blocks = selected.shape[0]
    layout = (blocks, piece_rows) + own_keys.shape[1:]
    wanted = jnp.transpose(selected)
    send_keys = held_keys.reshape(layout)[wanted]
    send_values = held_values.reshape(layout)[wanted]
    got_keys, got_values = (
        lax.all_to_all(send_keys, "ctx", split_axis=1, concat_axis=1, tiled=True),
        lax.all_to_all(send_values, "ctx", split_axis=1, concat_axis=1, tiled=True),
    )
    joined = (2, blocks * piece_rows) + own_keys.shape[1:]
    return (got_keys.reshape(joined), got_values.reshape(joined))


def return_home(part_keys, part_values, selected, piece_rows):
    blocks = selected.shape[0]
    rows_block = blocks * piece_rows
    trailing = part_keys.shape[1:]
    layout = (2, blocks, piece_rows) + trailing
    back_keys, back_values = (
        lax.all_to_all(
            part_keys[: 2 * rows_block].reshape(layout),
            "ctx",
            split_axis=1,
            concat_axis=1,
            tiled=True,
        ),
        lax.all_to_all(
            part_values[: 2 * rows_block].reshape(layout),
            "ctx",
            split_axis=1,
            concat_axis=1,
            tiled=True,
        ),
    )
    owners = (
        jnp.transpose(selected)[:, :, None] == jnp.arange(blocks, dtype=jnp.int32)[None, None, :]
    ).astype(jnp.float32)

    def collect(arrived):
        summed = jnp.einsum(
            "jrb,jrx->bx", owners, arrived.reshape(2, blocks, -1), precision=lax.Precision.HIGHEST
        )
        return summed.reshape((blocks, piece_rows) + trailing)

    home_keys, home_values = (
        lax.all_to_all(collect(back_keys), "ctx", split_axis=0, concat_axis=0, tiled=True),
        lax.all_to_all(collect(back_values), "ctx", split_axis=0, concat_axis=0, tiled=True),
    )
    own_rows = (rows_block,) + trailing
    return (
        home_keys.reshape(own_rows) + part_keys[2 * rows_block :],
        home_values.reshape(own_rows) + part_values[2 * rows_block :],
    )


def attend_head(queries_head, keys_head, values_head, grads_head, visible, softmax_scale):
    scores = (
        jnp.einsum("qgd,kd->gqk", queries_head, keys_head, preferred_element_type=jnp.float32)
        * softmax_scale
    )
    scores = jnp.where(visible[None], scores, -jnp.inf)
    row_max = jnp.max(scores, axis=-1, keepdims=True)
    weights = jnp.exp(scores - row_max)
    probs = weights / jnp.sum(weights, axis=-1, keepdims=True)
    probs_low = probs.astype(jnp.bfloat16)
    head_out = jnp.einsum(
        "gqk,kd->qgd", probs_low, values_head, preferred_element_type=jnp.float32
    ).astype(jnp.bfloat16)
    row_dot = jnp.sum(grads_head.astype(jnp.float32) * head_out.astype(jnp.float32), axis=-1)
    grad_probs = jnp.einsum(
        "qgd,kd->gqk", grads_head, values_head, preferred_element_type=jnp.float32
    )
    grad_scores = (
        probs * (grad_probs - jnp.transpose(row_dot)[:, :, None]) * softmax_scale
    ).astype(jnp.bfloat16)
    head_dq = jnp.einsum(
        "gqk,kd->qgd", grad_scores, keys_head, preferred_element_type=jnp.float32
    ).astype(jnp.bfloat16)
    head_dk = jnp.einsum(
        "gqk,qgd->kd", grad_scores, queries_head, preferred_element_type=jnp.float32
    )
    head_dv = jnp.einsum("gqk,qgd->kd", probs_low, grads_head, preferred_element_type=jnp.float32)
    return (head_out, head_dq, head_dk, head_dv)


def on_device(queries, keys, values, output_gradient, selected):
    rows_block = queries.shape[0]
    kv_count = keys.shape[1]
    head_size = keys.shape[2]
    piece_rows = rows_block // lax.axis_size("ctx")
    own_index = lax.axis_index("ctx")
    softmax_scale = head_size ** (-0.5)
    near_keys, near_values = fetch_blocks(keys, values, selected, piece_rows)
    all_keys = jnp.concatenate([near_keys[0], near_keys[1], keys], axis=0)
    all_values = jnp.concatenate([near_values[0], near_values[1], values], axis=0)
    own_picks = lax.dynamic_index_in_dim(selected, own_index, 0, keepdims=False)
    position = jnp.arange(rows_block, dtype=jnp.int32)
    causal = position[:, None] >= position[None, :]
    visible = jnp.concatenate(
        [
            jnp.broadcast_to(own_picks[0] < own_index, (rows_block, rows_block)),
            jnp.broadcast_to(own_picks[1] < own_index, (rows_block, rows_block)),
            causal,
        ],
        axis=1,
    )

    def per_head(head_pos, totals):
        attn_acc, dq_acc, dk_acc, dv_acc = totals
        head_out, head_dq, head_dk, head_dv = attend_head(
            lax.dynamic_index_in_dim(queries, head_pos, 2, keepdims=False),
            lax.dynamic_index_in_dim(all_keys, head_pos, 1, keepdims=False),
            lax.dynamic_index_in_dim(all_values, head_pos, 1, keepdims=False),
            lax.dynamic_index_in_dim(output_gradient, head_pos, 2, keepdims=False),
            visible,
            softmax_scale,
        )
        attn_acc = lax.dynamic_update_index_in_dim(attn_acc, head_out, head_pos, 2)
        dq_acc = lax.dynamic_update_index_in_dim(dq_acc, head_dq, head_pos, 2)
        dk_acc = lax.dynamic_update_index_in_dim(dk_acc, head_dk, head_pos, 1)
        dv_acc = lax.dynamic_update_index_in_dim(dv_acc, head_dv, head_pos, 1)
        return (attn_acc, dq_acc, dk_acc, dv_acc)

    initial = (
        jnp.zeros(queries.shape, jnp.bfloat16),
        jnp.zeros(queries.shape, jnp.bfloat16),
        jnp.zeros(all_keys.shape, jnp.float32),
        jnp.zeros(all_keys.shape, jnp.float32),
    )
    attn_out, grad_q, part_keys, part_values = lax.fori_loop(0, kv_count, per_head, initial)
    grad_keys, grad_values = return_home(part_keys, part_values, selected, piece_rows)
    grad_keys, grad_values = (
        lax.psum_scatter(grad_keys, "head", scatter_dimension=1, tiled=True),
        lax.psum_scatter(grad_values, "head", scatter_dimension=1, tiled=True),
    )
    return (attn_out, grad_q, grad_keys.astype(jnp.bfloat16), grad_values.astype(jnp.bfloat16))


def solution(mesh):
    return jax.shard_map(
        on_device,
        mesh=mesh,
        in_specs=(
            P("ctx", "head", None, None),
            P("ctx", None, None),
            P("ctx", None, None),
            P("ctx", "head", None, None),
            P(),
        ),
        out_specs=(
            P("ctx", "head", None, None),
            P("ctx", "head", None, None),
            P("ctx", "head", None),
            P("ctx", "head", None),
        ),
        check_vma=False,
    )
```

profile of v0, /device:TPU:0, one launch (start us, length us, event | category | flops | bytes accessed | tf_op | source)
XLA Modules:
  0.0 373.0 jit_solution(18032600717242512195)
XLA Ops:
  7.2 23.4 %all_to_all.40 = bf16[512,4,128]{2,1,0:T(4,128)(2,1)S(1)} all-to-all(bf16[512,4,128]{2,1,0:T(4,128)(2,1)} %param.9), channel_id=1, replica_groups=mesh['ctx'=16,'head'=2] {'ctx'}, dimensions={0} | all-to-all | bytes 1048576 | tf_op jit(solution)/shard_map/all_to_all | solution.py:10
  30.6 3.9 %all-to-all-start.2 = ((bf16[512,4,128]{2,1,0:T(4,128)(2,1)}), bf16[512,4,128]{2,1,0:T(4,128)(2,1)S(1)}, u32[]{:S(2)}, u32[]{:S(2)}) async-start(bf16[512,4,128]{2,1,0:T(4,128)(2,1)} %param.8), calls=%async_computation.2 | async-start | bytes 1048576 | tf_op jit(solution)/shard_map/all_to_all | solution.py:9
  37.3 11.7 %all-to-all-done.2 = bf16[512,4,128]{2,1,0:T(4,128)(2,1)S(1)} async-done(((bf16[512,4,128]{2,1,0:T(4,128)(2,1)}), bf16[512,4,128]{2,1,0:T(4,128)(2,1)S(1)}, u32[]{:S(2)}, u32[]{:S(2)}) %all-to-all-start.2) | async-done | bytes 524320 | tf_op jit(solution)/shard_map/all_to_all | solution.py:9
  49.0 3.9 %all-to-all-start.1 = ((bf16[2,16,32,4,128]{4,2,3,0,1:T(8,128)(2,1)}), bf16[2,16,32,4,128]{4,2,3,0,1:T(8,128)(2,1)S(1)}, u32[]{:S(2)}, u32[]{:S(2)}) async-start(bf16[2,16,32,4,128]{4,2,3,0,1:T(8,128)(2,1)} %copy.141), calls=%async_computation.1 | async-start | bytes 2097152 | tf_op jit(solution)/shard_map/all_to_all | solution.py:19
  54.8 21.7 %all-to-all-done.1 = bf16[2,16,32,4,128]{4,2,3,0,1:T(8,128)(2,1)S(1)} async-done(((bf16[2,16,32,4,128]{4,2,3,0,1:T(8,128)(2,1)}), bf16[2,16,32,4,128]{4,2,3,0,1:T(8,128)(2,1)S(1)}, u32[]{:S(2)}, u32[]{:S(2)}) %all-to-all-start.1) | async-done | bytes 1048608 | tf_op jit(solution)/shard_map/all_to_all | solution.py:19
  76.5 5.9 %all-to-all-start.3 = ((bf16[2,16,32,4,128]{4,2,3,0,1:T(8,128)(2,1)}), bf16[2,16,32,4,128]{4,2,3,0,1:T(8,128)(2,1)S(1)}, u32[]{:S(2)}, u32[]{:S(2)}) async-start(bf16[2,16,32,4,128]{4,2,3,0,1:T(8,128)(2,1)} %copy.147), calls=%async_computation.3 | async-start | bytes 2097152 | tf_op jit(solution)/shard_map/all_to_all | solution.py:18
  86.1 2.3 copy.152
  88.4 1.6 copy.153
  90.2 2.2 pad_add_fusion
  94.2 11.1 %all-to-all-done.3 = bf16[2,16,32,4,128]{4,2,3,0,1:T(8,128)(2,1)S(1)} async-done(((bf16[2,16,32,4,128]{4,2,3,0,1:T(8,128)(2,1)}), bf16[2,16,32,4,128]{4,2,3,0,1:T(8,128)(2,1)S(1)}, u32[]{:S(2)}, u32[]{:S(2)}) %all-to-all-start.3) | async-done | bytes 1048608 | tf_op jit(solution)/shard_map/all_to_all | solution.py:18
  106.5 2.4 pad_maximum_fusion
  108.9 75.0 %while.19 = (s32[]{:T(128)}, bf16[512,2,4,128]{0,3,1,2:T(8,128)(2,1)}, bf16[512,2,4,128]{0,3,1,2:T(8,128)(2,1)}, f32[1536,4,128]{2,0,1:T(8,128)}, f32[1536,4,128...) while((s32[]{:T(128)}, ...), condition=%wide.region_4.5_spmd, body=%wide.region_0.4_spmd.sunk | while | flops 2434007552 | bytes 79718664 | solution.py:141
  108.9 6.1 %fusion.107 = (f32[2,512]{1,0:T(2,128)S(1)}, f32[2,512,1536]{1,2,0:T(8,128)}) fusion(pred[512,1536]{0,1:T(8,128)(4,1)S(1)} %get-tuple-element.393, bf16[1536,4,128]{2,0,1:T(8,128)(2,1)} %get-tuple-element.394, s32[]{:T(128)} %get-tuple-element.376, bf16[512,2,4,128]{3,0,1,2:T(8,128)(2,1)} %get-tuple-element.395), kind=kOutput, calls=%fused_computation.78.clone.1 | convolution fusion | flops 408946176 | bytes 7738368 | tf_op jit(solution)/shard_map/while/body/eval_jaxpr/sub | solution.py:74
  115.1 3.9 %fusion.108 = bf16[2,512,1536]{1,2,0:T(8,128)(2,1)S(1)} fusion(f32[2,512,1536]{1,2,0:T(8,128)} %get-tuple-element.361, f32[2,512]{1,0:T(2,128)S(1)} %get-tuple-element.362), kind=kLoop, calls=%fused_computation.14.clone.1 | loop fusion | flops 3145728 | bytes 9441280 | tf_op jit(solution)/shard_map/while/body/eval_jaxpr/convert_element_type | solution.py:76
  120.0 1.2 fusion.109
  121.2 2.9 fusion.111
  124.1 1.6 fusion.110
  125.8 1.9 fusion.112
  127.6 6.1 %fusion.107 = (f32[2,512]{1,0:T(2,128)S(1)}, f32[2,512,1536]{1,2,0:T(8,128)}) fusion(pred[512,1536]{0,1:T(8,128)(4,1)S(1)} %get-tuple-element.393, bf16[1536,4,128]{2,0,1:T(8,128)(2,1)} %get-tuple-element.394, s32[]{:T(128)} %get-tuple-element.376, bf16[512,2,4,128]{3,0,1,2:T(8,128)(2,1)} %get-tuple-element.395), kind=kOutput, calls=%fused_computation.78.clone.1 | convolution fusion | flops 408946176 | bytes 7738368 | tf_op jit(solution)/shard_map/while/body/eval_jaxpr/sub | solution.py:74
  133.8 3.9 %fusion.108 = bf16[2,512,1536]{1,2,0:T(8,128)(2,1)S(1)} fusion(f32[2,512,1536]{1,2,0:T(8,128)} %get-tuple-element.361, f32[2,512]{1,0:T(2,128)S(1)} %get-tuple-element.362), kind=kLoop, calls=%fused_computation.14.clone.1 | loop fusion | flops 3145728 | bytes 9441280 | tf_op jit(solution)/shard_map/while/body/eval_jaxpr/convert_element_type | solution.py:76
  138.7 1.2 fusion.109
  139.9 2.9 fusion.111
  142.9 1.6 fusion.110
  144.5 1.9 fusion.112
  146.4 6.1 %fusion.107 = (f32[2,512]{1,0:T(2,128)S(1)}, f32[2,512,1536]{1,2,0:T(8,128)}) fusion(pred[512,1536]{0,1:T(8,128)(4,1)S(1)} %get-tuple-element.393, bf16[1536,4,128]{2,0,1:T(8,128)(2,1)} %get-tuple-element.394, s32[]{:T(128)} %get-tuple-element.376, bf16[512,2,4,128]{3,0,1,2:T(8,128)(2,1)} %get-tuple-element.395), kind=kOutput, calls=%fused_computation.78.clone.1 | convolution fusion | flops 408946176 | bytes 7738368 | tf_op jit(solution)/shard_map/while/body/eval_jaxpr/sub | solution.py:74
  152.5 3.9 %fusion.108 = bf16[2,512,1536]{1,2,0:T(8,128)(2,1)S(1)} fusion(f32[2,512,1536]{1,2,0:T(8,128)} %get-tuple-element.361, f32[2,512]{1,0:T(2,128)S(1)} %get-tuple-element.362), kind=kLoop, calls=%fused_computation.14.clone.1 | loop fusion | flops 3145728 | bytes 9441280 | tf_op jit(solution)/shard_map/while/body/eval_jaxpr/convert_element_type | solution.py:76
  157.5 1.2 fusion.109
  158.7 3.0 fusion.111
  161.6 1.6 fusion.110
  163.3 1.9 fusion.112
  165.1 6.1 %fusion.107 = (f32[2,512]{1,0:T(2,128)S(1)}, f32[2,512,1536]{1,2,0:T(8,128)}) fusion(pred[512,1536]{0,1:T(8,128)(4,1)S(1)} %get-tuple-element.393, bf16[1536,4,128]{2,0,1:T(8,128)(2,1)} %get-tuple-element.394, s32[]{:T(128)} %get-tuple-element.376, bf16[512,2,4,128]{3,0,1,2:T(8,128)(2,1)} %get-tuple-element.395), kind=kOutput, calls=%fused_computation.78.clone.1 | convolution fusion | flops 408946176 | bytes 7738368 | tf_op jit(solution)/shard_map/while/body/eval_jaxpr/sub | solution.py:74
  171.3 3.9 %fusion.108 = bf16[2,512,1536]{1,2,0:T(8,128)(2,1)S(1)} fusion(f32[2,512,1536]{1,2,0:T(8,128)} %get-tuple-element.361, f32[2,512]{1,0:T(2,128)S(1)} %get-tuple-element.362), kind=kLoop, calls=%fused_computation.14.clone.1 | loop fusion | flops 3145728 | bytes 9441280 | tf_op jit(solution)/shard_map/while/body/eval_jaxpr/convert_element_type | solution.py:76
  176.3 1.2 fusion.109
  177.5 2.9 fusion.111
  180.4 1.6 fusion.110
  182.0 1.9 fusion.112
  183.9 1.7 slice.44
  185.6 3.1 copy.159
  188.7 6.0 %all-to-all-start.6 = ((f32[2,16,32,4,128]{4,3,2,0,1:T(4,128)}), f32[2,16,32,4,128]{4,3,2,0,1:T(4,128)S(1)}, u32[]{:S(2)}, u32[]{:S(2)}) async-start(f32[2,16,32,4,128]{4,3,2,0,1:T(4,128)} %copy.159), calls=%async_computation.7 | async-start | bytes 4194304 | tf_op jit(solution)/shard_map/all_to_all | solution.py:38
  194.8 1.7 slice.42
  196.5 3.1 copy.154
  199.6 36.9 %all-to-all-done.6 = f32[2,16,32,4,128]{4,3,2,0,1:T(4,128)S(1)} async-done(((f32[2,16,32,4,128]{4,3,2,0,1:T(4,128)}), f32[2,16,32,4,128]{4,3,2,0,1:T(4,128)S(1)}, u32[]{:S(2)}, u32[]{:S(2)}) %all-to-all-start.6) | async-done | bytes 2097184 | tf_op jit(solution)/shard_map/all_to_all | solution.py:38
  236.5 1.4 copy-done
  237.9 9.8 %all-to-all-start.4 = ((f32[2,16,32,4,128]{4,3,2,0,1:T(4,128)}), f32[2,16,32,4,128]{4,3,2,0,1:T(4,128)S(1)}, u32[]{:S(2)}, u32[]{:S(2)}) async-start(f32[2,16,32,4,128]{4,3,2,0,1:T(4,128)} %copy.154), calls=%async_computation.4 | async-start | bytes 4194304 | tf_op jit(solution)/shard_map/all_to_all | solution.py:31
  247.7 3.9 %reshape.93 = f32[2,16,16384]{2,0,1:T(2,128)} reshape(f32[2,16,32,4,128]{4,3,2,0,1:T(4,128)} %copy-done) | data formatting | bytes 4194304 | tf_op jit(solution)/shard_map/reshape | solution.py:52
  251.6 4.2 %copy.200 = f32[2,16,16384]{2,1,0:T(8,128)} copy(f32[2,16,16384]{2,0,1:T(2,128)} %reshape.93) | data formatting | bytes 4194304 | tf_op jit(solution)/shard_map/reshape | solution.py:52
  255.7 3.6 dot_general.60
  259.4 3.5 fusion.59
  262.9 1.4 copy.162
  264.3 25.9 %all-to-all-done.4 = f32[2,16,32,4,128]{4,3,2,0,1:T(4,128)S(1)} async-done(((f32[2,16,32,4,128]{4,3,2,0,1:T(4,128)}), f32[2,16,32,4,128]{4,3,2,0,1:T(4,128)S(1)}, u32[]{:S(2)}, u32[]{:S(2)}) %all-to-all-start.4) | async-done | bytes 2097184 | tf_op jit(solution)/shard_map/all_to_all | solution.py:31
  290.2 9.8 %all-to-all-start.7 = ((f32[16,32,4,128]{3,2,1,0:T(4,128)}), f32[16,32,4,128]{3,2,1,0:T(4,128)S(1)}, u32[]{:S(2)}, u32[]{:S(2)}) async-start(f32[16,32,4,128]{3,2,1,0:T(4,128)} %copy.162), calls=%async_computation.8 | async-start | bytes 2097152 | tf_op jit(solution)/shard_map/all_to_all | solution.py:58
  300.0 2.7 reshape.92
  302.7 2.8 copy.201
  305.5 2.4 dot_general.57
  307.9 3.5 fusion.56
  311.4 1.4 copy.157
  312.8 10.9 %all-to-all-done.7 = f32[16,32,4,128]{3,2,1,0:T(4,128)S(1)} async-done(((f32[16,32,4,128]{3,2,1,0:T(4,128)}), f32[16,32,4,128]{3,2,1,0:T(4,128)S(1)}, u32[]{:S(2)}, u32[]{:S(2)}) %all-to-all-start.7) | async-done | bytes 1048608 | tf_op jit(solution)/shard_map/all_to_all | solution.py:58
  323.7 5.9 %all-to-all-start.5 = ((f32[16,32,4,128]{3,2,1,0:T(4,128)}), f32[16,32,4,128]{3,2,1,0:T(4,128)S(1)}, u32[]{:S(2)}, u32[]{:S(2)}) async-start(f32[16,32,4,128]{3,2,1,0:T(4,128)} %copy.157), calls=%async_computation.5 | async-start | bytes 2097152 | tf_op jit(solution)/shard_map/all_to_all | solution.py:57
  329.7 2.4 bitcast_add_fusion
  332.2 20.3 %all-to-all-done.5 = f32[16,32,4,128]{3,2,1,0:T(4,128)S(1)} async-done(((f32[16,32,4,128]{3,2,1,0:T(4,128)}), f32[16,32,4,128]{3,2,1,0:T(4,128)S(1)}, u32[]{:S(2)}, u32[]{:S(2)}) %all-to-all-start.5) | async-done | bytes 1048608 | tf_op jit(solution)/shard_map/all_to_all | solution.py:57
  352.7 2.4 bitcast_add_fusion.1
  355.1 1.5 copy.164
  356.6 1.5 copy.165
  360.1 3.9 %reduce-scatter.3.cloned.1.call-done = f32[512,2,128]{2,0,1:T(8,128)} async-done(((f32[512,4,128]{2,0,1:T(8,128)}), f32[512,2,128]{2,0,1:T(8,128)}) %reduce-scatter.3.cloned.1.call-update) | async-done | bytes 524304 | tf_op jit(solution)/shard_map/reduce_scatter | solution.py:144
  (115 shorter events, 18.9 us)
Async XLA Ops:
  30.6 18.4 %all-to-all-start.2 = ((bf16[512,4,128]{2,1,0:T(4,128)(2,1)}), bf16[512,4,128]{2,1,0:T(4,128)(2,1)S(1)}, u32[]{:S(2)}, u32[]{:S(2)}) async-start(bf16[512,4,128]{2,1,0:T(4,128)(2,1)} %param.8), calls=%async_computation.2 | async-start | bytes 1048576 | tf_op jit(solution)/shard_map/all_to_all | solution.py:9
  49.0 27.5 %all-to-all-start.1 = ((bf16[2,16,32,4,128]{4,2,3,0,1:T(8,128)(2,1)}), bf16[2,16,32,4,128]{4,2,3,0,1:T(8,128)(2,1)S(1)}, u32[]{:S(2)}, u32[]{:S(2)}) async-start(bf16[2,16,32,4,128]{4,2,3,0,1:T(8,128)(2,1)} %copy.141), calls=%async_computation.1 | async-start | bytes 2097152 | tf_op jit(solution)/shard_map/all_to_all | solution.py:19
  53.0 29.4 %copy-start.3 = (bf16[512,4,128]{2,1,0:T(4,128)(2,1)S(1)}, bf16[512,4,128]{2,1,0:T(4,128)(2,1)}, u32[]{:S(2)}) copy-start(bf16[512,4,128]{2,1,0:T(4,128)(2,1)} %param.9) | copy-start | bytes 1572868
  53.8 29.5 %copy-start.4 = (bf16[512,4,128]{2,1,0:T(4,128)(2,1)S(1)}, bf16[512,4,128]{2,1,0:T(4,128)(2,1)}, u32[]{:S(2)}) copy-start(bf16[512,4,128]{2,1,0:T(4,128)(2,1)} %param.8) | copy-start | bytes 1572868
  53.8 30.4 %copy-start.12 = (s32[16,2]{0,1:T(2,128)S(1)}, s32[16,2]{0,1:T(2,128)}, u32[]{:S(2)}) copy-start(s32[16,2]{0,1:T(2,128)} %param.11) | copy-start | bytes 388
  76.5 28.8 %all-to-all-start.3 = ((bf16[2,16,32,4,128]{4,2,3,0,1:T(8,128)(2,1)}), bf16[2,16,32,4,128]{4,2,3,0,1:T(8,128)(2,1)S(1)}, u32[]{:S(2)}, u32[]{:S(2)}) async-start(bf16[2,16,32,4,128]{4,2,3,0,1:T(8,128)(2,1)} %copy.147), calls=%async_computation.3 | async-start | bytes 2097152 | tf_op jit(solution)/shard_map/all_to_all | solution.py:18
  105.3 1.0 copy-start.1
  105.3 1.2 copy-start.2
  106.5 2.4 copy-start.11
  115.0 4.6 %slice-start = ((s8[6291456]{0:T(1024)(128)(4,1)}), s8[4194304]{0:T(1024)(128)(4,1)S(1)}, s32[]{:S(2)}) async-start(s8[6291456]{0:T(1024)(128)(4,1)} %bitcast.170), calls=%async_computation.12 | async-start | bytes 8388608 | tf_op jit(solution)/shard_map/while
  115.0 3.9 %copy-start.5 = (bf16[512,2,4,128]{0,3,1,2:T(8,128)(2,1)S(1)}, bf16[512,2,4,128]{0,3,1,2:T(8,128)(2,1)}, u32[]{:S(2)}) copy-start(bf16[512,2,4,128]{0,3,1,2:T(8,128)(2,1)} %get-tuple-element.377) | copy-start | bytes 3145732 | tf_op jit(solution)/shard_map/while
  115.0 5.0 %slice-start.1 = ((s8[6291456]{0:T(1024)(128)(4,1)}), s8[2097152]{0:T(1024)(128)(4,1)S(1)}, s32[]{:S(2)}) async-start(s8[6291456]{0:T(1024)(128)(4,1)} %bitcast.170), calls=%async_computation.13 | async-start | bytes 4194304 | tf_op jit(solution)/shard_map/while
  119.6 1.6 copy-start.6
  121.2 2.9 copy-start.8
  125.8 1.9 copy-start.9
  133.8 4.6 %slice-start = ((s8[6291456]{0:T(1024)(128)(4,1)}), s8[4194304]{0:T(1024)(128)(4,1)S(1)}, s32[]{:S(2)}) async-start(s8[6291456]{0:T(1024)(128)(4,1)} %bitcast.170), calls=%async_computation.12 | async-start | bytes 8388608 | tf_op jit(solution)/shard_map/while
  133.8 3.9 %copy-start.5 = (bf16[512,2,4,128]{0,3,1,2:T(8,128)(2,1)S(1)}, bf16[512,2,4,128]{0,3,1,2:T(8,128)(2,1)}, u32[]{:S(2)}) copy-start(bf16[512,2,4,128]{0,3,1,2:T(8,128)(2,1)} %get-tuple-element.377) | copy-start | bytes 3145732 | tf_op jit(solution)/shard_map/while
  133.8 5.0 %slice-start.1 = ((s8[6291456]{0:T(1024)(128)(4,1)}), s8[2097152]{0:T(1024)(128)(4,1)S(1)}, s32[]{:S(2)}) async-start(s8[6291456]{0:T(1024)(128)(4,1)} %bitcast.170), calls=%async_computation.13 | async-start | bytes 4194304 | tf_op jit(solution)/shard_map/while
  138.3 1.7 copy-start.6
  139.9 2.9 copy-start.8
  144.5 1.9 copy-start.9
  152.5 4.6 %slice-start = ((s8[6291456]{0:T(1024)(128)(4,1)}), s8[4194304]{0:T(1024)(128)(4,1)S(1)}, s32[]{:S(2)}) async-start(s8[6291456]{0:T(1024)(128)(4,1)} %bitcast.170), calls=%async_computation.12 | async-start | bytes 8388608 | tf_op jit(solution)/shard_map/while
  152.5 3.9 %copy-start.5 = (bf16[512,2,4,128]{0,3,1,2:T(8,128)(2,1)S(1)}, bf16[512,2,4,128]{0,3,1,2:T(8,128)(2,1)}, u32[]{:S(2)}) copy-start(bf16[512,2,4,128]{0,3,1,2:T(8,128)(2,1)} %get-tuple-element.377) | copy-start | bytes 3145732 | tf_op jit(solution)/shard_map/while
  152.5 5.0 %slice-start.1 = ((s8[6291456]{0:T(1024)(128)(4,1)}), s8[2097152]{0:T(1024)(128)(4,1)S(1)}, s32[]{:S(2)}) async-start(s8[6291456]{0:T(1024)(128)(4,1)} %bitcast.170), calls=%async_computation.13 | async-start | bytes 4194304 | tf_op jit(solution)/shard_map/while
  157.0 1.7 copy-start.6
  158.7 3.0 copy-start.8
  163.3 1.9 copy-start.9
  171.3 4.6 %slice-start = ((s8[6291456]{0:T(1024)(128)(4,1)}), s8[4194304]{0:T(1024)(128)(4,1)S(1)}, s32[]{:S(2)}) async-start(s8[6291456]{0:T(1024)(128)(4,1)} %bitcast.170), calls=%async_computation.12 | async-start | bytes 8388608 | tf_op jit(solution)/shard_map/while
  171.3 3.9 %copy-start.5 = (bf16[512,2,4,128]{0,3,1,2:T(8,128)(2,1)S(1)}, bf16[512,2,4,128]{0,3,1,2:T(8,128)(2,1)}, u32[]{:S(2)}) copy-start(bf16[512,2,4,128]{0,3,1,2:T(8,128)(2,1)} %get-tuple-element.377) | copy-start | bytes 3145732 | tf_op jit(solution)/shard_map/while
  171.3 5.0 %slice-start.1 = ((s8[6291456]{0:T(1024)(128)(4,1)}), s8[2097152]{0:T(1024)(128)(4,1)S(1)}, s32[]{:S(2)}) async-start(s8[6291456]{0:T(1024)(128)(4,1)} %bitcast.170), calls=%async_computation.13 | async-start | bytes 4194304 | tf_op jit(solution)/shard_map/while
  175.8 1.7 copy-start.6
  177.5 2.9 copy-start.8
  182.0 1.9 copy-start.9
  188.7 47.8 %all-to-all-start.6 = ((f32[2,16,32,4,128]{4,3,2,0,1:T(4,128)}), f32[2,16,32,4,128]{4,3,2,0,1:T(4,128)S(1)}, u32[]{:S(2)}, u32[]{:S(2)}) async-start(f32[2,16,32,4,128]{4,3,2,0,1:T(4,128)} %copy.159), calls=%async_computation.7 | async-start | bytes 4194304 | tf_op jit(solution)/shard_map/all_to_all | solution.py:38
  236.5 1.4 copy-start
  237.9 52.3 %all-to-all-start.4 = ((f32[2,16,32,4,128]{4,3,2,0,1:T(4,128)}), f32[2,16,32,4,128]{4,3,2,0,1:T(4,128)S(1)}, u32[]{:S(2)}, u32[]{:S(2)}) async-start(f32[2,16,32,4,128]{4,3,2,0,1:T(4,128)} %copy.154), calls=%async_computation.4 | async-start | bytes 4194304 | tf_op jit(solution)/shard_map/all_to_all | solution.py:31
  290.2 33.5 %all-to-all-start.7 = ((f32[16,32,4,128]{3,2,1,0:T(4,128)}), f32[16,32,4,128]{3,2,1,0:T(4,128)S(1)}, u32[]{:S(2)}, u32[]{:S(2)}) async-start(f32[16,32,4,128]{3,2,1,0:T(4,128)} %copy.162), calls=%async_computation.8 | async-start | bytes 2097152 | tf_op jit(solution)/shard_map/all_to_all | solution.py:58
  323.7 28.8 %all-to-all-start.5 = ((f32[16,32,4,128]{3,2,1,0:T(4,128)}), f32[16,32,4,128]{3,2,1,0:T(4,128)S(1)}, u32[]{:S(2)}, u32[]{:S(2)}) async-start(f32[16,32,4,128]{3,2,1,0:T(4,128)} %copy.157), calls=%async_computation.5 | async-start | bytes 2097152 | tf_op jit(solution)/shard_map/all_to_all | solution.py:57
  329.5 28.5 %reduce-scatter.5.cloned.1.call-start = ((), (), s32[]{:S(2)}) async-start(), calls=%async_computation.11 | async-start | bytes 1572864 | tf_op jit(solution)/shard_map/reduce_scatter | solution.py:145
  332.2 23.0 %copy-start.7 = (bf16[512,2,4,128]{0,3,1,2:T(8,128)(2,1)S(1)}, bf16[512,2,4,128]{0,3,1,2:T(8,128)(2,1)}, u32[]{:S(2)}) copy-start(bf16[512,2,4,128]{0,3,1,2:T(8,128)(2,1)} %get-tuple-element.260) | copy-start | bytes 3145732
  332.2 31.9 %reduce-scatter.3.cloned.1.call-start = ((), (), s32[]{:S(2)}) async-start(), calls=%async_computation.10 | async-start | bytes 1572864 | tf_op jit(solution)/shard_map/reduce_scatter | solution.py:144
  352.7 4.0 %copy-start.10 = (bf16[512,2,4,128]{0,3,1,2:T(8,128)(2,1)S(1)}, bf16[512,2,4,128]{0,3,1,2:T(8,128)(2,1)}, u32[]{:S(2)}) copy-start(bf16[512,2,4,128]{0,3,1,2:T(8,128)(2,1)} %get-tuple-element.261) | copy-start | bytes 3145732
Sparse Core Ops, SparseCore 0:
  332.6 9.6 reduce-scatter.4
  355.2 8.7 reduce-scatter.2
where the time goes:
time: 375 us; the launch traced here: 373 us
  waiting for transfers between devices  142 us (38%)
  matrix products  64.4 us (17%)
  local copies, waits for them, and re-layouts  53.3 us (14%)
  starting transfers between devices  45.3 us (12%)
  other arithmetic  28.3 us (8%)
  blocking collectives  23.4 us (6%)
  between operations  15.6 us (4%)
    all_to_all x1, waiting for transfers between devices, return_home(): lax.all_to_all(part_values[:2 * rows_block].reshape(layout), 'ctx', split...  36.9 us
    all_to_all x1, waiting for transfers between devices, return_home(): lax.all_to_all(part_keys[:2 * rows_block].reshape(layout), 'ctx', split_a...  25.9 us
    sub x4, matrix products, attend_head(): weights = jnp.exp(scores - row_max)  24.5 us
    all_to_all x1, blocking collectives, fetch_blocks(): lax.all_to_all(own_values, 'ctx', split_axis=0, concat_axis=0, tiled=True)  23.4 us
    all_to_all x1, waiting for transfers between devices, fetch_blocks(): lax.all_to_all(send_values, 'ctx', split_axis=1, concat_axis=1, tiled=True)  21.7 us
    all_to_all x1, waiting for transfers between devices, return_home(): lax.all_to_all(collect(back_keys), 'ctx', split_axis=0, concat_axis=0, ti...  20.3 us
    convert_element_type x4, other arithmetic, attend_head(): probs_low = probs.astype(jnp.bfloat16)  15.5 us
    reshape x4, local copies, waits for them, and re-layouts, collect(): arrived.reshape(2, blocks, -1)  13.6 us
  transfers between devices with their start and end apart: 9, of which 8 were waited for; matrix products, arithmetic and copies ran while one was open for 16% of the time, Pallas kernels for 0%

commit v1 on v0

--- a/solution.py
+++ b/solution.py
@@ -16,7 +16,12 @@
     send_values = held_values.reshape(layout)[wanted]
     got_keys, got_values = (
         lax.all_to_all(send_keys, "ctx", split_axis=1, concat_axis=1, tiled=True),
-        lax.all_to_all(send_values, "ctx", split_axis=1, concat_axis=1, tiled=True),
+        jnp.concatenate(
+            lax.all_to_all(
+                jnp.stack(jnp.split(send_values, lax.axis_size("ctx"), axis=1)), "ctx", 0, 0
+            ),
+            axis=1,
+        ),
     )
     joined = (2, blocks * piece_rows) + own_keys.shape[1:]
     return (got_keys.reshape(joined), got_values.reshape(joined))

time: 375 us -> 375 us (level)
  blocking collectives: 23.4 us -> 0 us
  local copies, waits for them, and re-layouts: 53.3 us -> 62.5 us
  starting transfers between devices: 45.3 us -> 53.6 us
  waiting for transfers between devices: 142 us -> 148 us
    all_to_all x1 -> x0, blocking collectives: 23.4 us -> none  [fetch_blocks(): lax.all_to_all(own_values, 'ctx', split_axis=0, concat_axis=0, tiled=True)]
    all_to_all x1 -> x2, waiting for transfers between devices: 21.7 us -> 36 us  [the longest x1 21.7 us: fetch_blocks(): lax.all_to_all(jnp.stack(jnp.split(send_values, lax.axis_size('ctx'), axi...]
    all_to_all x1 -> x2, starting transfers between devices: 3.88 us -> 12.2 us  [the longest x1 8.35 us: fetch_blocks(): lax.all_to_all(own_values, 'ctx', split_axis=0, concat_axis=0, tiled=True)]
    all_to_all x1, waiting for transfers between devices: 11.7 us -> 3.4 us  [fetch_blocks(): lax.all_to_all(own_keys, 'ctx', split_axis=0, concat_axis=0, tiled=True)]
    unnamed x28 -> x41, local copies, waits for them, and re-layouts: 10.9 us -> 18.6 us
  transfers between devices with their start and end apart: 9 -> 10, of which waited for: 8 -> 9; matrix products, arithmetic and copies ran while one was open for 16% -> 18% of each run, Pallas kernels for 0% -> 0%
where the time goes in v1:
time: 375 us; the launch traced here: 373 us
  waiting for transfers between devices  148 us (39%)
  matrix products  64.3 us (17%)
  local copies, waits for them, and re-layouts  62.5 us (17%)
  starting transfers between devices  53.6 us (14%)
  other arithmetic  28.3 us (8%)
  between operations  15.7 us (4%)
    all_to_all x1, waiting for transfers between devices, return_home(): lax.all_to_all(part_values[:2 * rows_block].reshape(layout), 'ctx', split...  36.9 us
    all_to_all x1, waiting for transfers between devices, return_home(): lax.all_to_all(part_keys[:2 * rows_block].reshape(layout), 'ctx', split_a...  25.9 us
    sub x4, matrix products, attend_head(): weights = jnp.exp(scores - row_max)  24.4 us
    all_to_all x1, waiting for transfers between devices, fetch_blocks(): lax.all_to_all(jnp.stack(jnp.split(send_values, lax.axis_size('ctx'), axi...  21.7 us
    all_to_all x1, waiting for transfers between devices, return_home(): lax.all_to_all(collect(back_keys), 'ctx', split_axis=0, concat_axis=0, ti...  20.3 us
    unnamed x41, local copies, waits for them, and re-layouts  18.6 us
    convert_element_type x4, other arithmetic, attend_head(): probs_low = probs.astype(jnp.bfloat16)  15.5 us
    all_to_all x1, waiting for transfers between devices, fetch_blocks(): lax.all_to_all(own_values, 'ctx', split_axis=0, concat_axis=0, tiled=True)  14.3 us
  transfers between devices with their start and end apart: 10, of which 9 were waited for; matrix products, arithmetic and copies ran while one was open for 18% of the time, Pallas kernels for 0%

profile of v1, /device:TPU:0, one launch (start us, length us, event | category | flops | bytes accessed | tf_op | source)
XLA Modules:
  0.0 372.9 jit_solution(11197950703657526468)
XLA Ops:
  7.2 8.4 %all-to-all-start = ((bf16[512,4,128]{2,1,0:T(4,128)(2,1)}), bf16[512,4,128]{2,1,0:T(4,128)(2,1)S(1)}, u32[]{:S(2)}, u32[]{:S(2)}) async-start(bf16[512,4,128]{2,1,0:T(4,128)(2,1)} %param.9), calls=%async_computation | async-start | bytes 1048576 | tf_op jit(solution)/shard_map/all_to_all | solution.py:10
  16.3 14.3 %all-to-all-done = bf16[512,4,128]{2,1,0:T(4,128)(2,1)S(1)} async-done(((bf16[512,4,128]{2,1,0:T(4,128)(2,1)}), bf16[512,4,128]{2,1,0:T(4,128)(2,1)S(1)}, u32[]{:S(2)}, u32[]{:S(2)}) %all-to-all-start) | async-done | bytes 524320 | tf_op jit(solution)/shard_map/all_to_all | solution.py:10
  30.6 3.9 %all-to-all-start.2 = ((bf16[512,4,128]{2,1,0:T(4,128)(2,1)}), bf16[512,4,128]{2,1,0:T(4,128)(2,1)S(1)}, u32[]{:S(2)}, u32[]{:S(2)}) async-start(bf16[512,4,128]{2,1,0:T(4,128)(2,1)} %param.8), calls=%async_computation.2 | async-start | bytes 1048576 | tf_op jit(solution)/shard_map/all_to_all | solution.py:9
  45.6 3.4 all-to-all-done.2
  49.0 3.9 %all-to-all-start.1 = ((bf16[16,2,1,32,4,128]{5,3,4,1,2,0:T(8,128)(2,1)}), bf16[16,2,1,32,4,128]{5,3,4,1,2,0:T(8,128)(2,1)S(1)}, u32[]{:S(2)}, u32[]{:S(2)}) async-start(bf16[16,2,1,32,4,128]{5,3,4,1,2,0:T(8,128)(2,1)} %fusion.62), calls=%async_computation.1 | async-start | bytes 2097152 | tf_op jit(solution)/shard_map/all_to_all | solution.py:20
  54.8 21.7 %all-to-all-done.1 = bf16[16,2,1,32,4,128]{5,3,4,1,2,0:T(8,128)(2,1)S(1)} async-done(((bf16[16,2,1,32,4,128]{5,3,4,1,2,0:T(8,128)(2,1)}), bf16[16,2,1,32,4,128]{5,3,4,1,2,0:T(8,128)(2,1)S(1)}, u32[]{:S(2)}, u32[]{:S(2)}) %all-to-all-start.1) | async-done | bytes 1048608 | tf_op jit(solution)/shard_map/all_to_all | solution.py:20
  76.5 5.9 %all-to-all-start.3 = ((bf16[2,16,32,4,128]{4,2,3,0,1:T(8,128)(2,1)}), bf16[2,16,32,4,128]{4,2,3,0,1:T(8,128)(2,1)S(1)}, u32[]{:S(2)}, u32[]{:S(2)}) async-start(bf16[2,16,32,4,128]{4,2,3,0,1:T(8,128)(2,1)} %copy.235), calls=%async_computation.3 | async-start | bytes 2097152 | tf_op jit(solution)/shard_map/all_to_all | solution.py:18
  86.2 2.3 copy.240
  88.5 1.6 copy.241
  90.3 2.2 pad_add_fusion
  94.4 11.0 %all-to-all-done.3 = bf16[2,16,32,4,128]{4,2,3,0,1:T(8,128)(2,1)S(1)} async-done(((bf16[2,16,32,4,128]{4,2,3,0,1:T(8,128)(2,1)}), bf16[2,16,32,4,128]{4,2,3,0,1:T(8,128)(2,1)S(1)}, u32[]{:S(2)}, u32[]{:S(2)}) %all-to-all-start.3) | async-done | bytes 1048608 | tf_op jit(solution)/shard_map/all_to_all | solution.py:18
  106.6 2.4 pad_maximum_fusion
  108.9 74.9 %while.19 = (s32[]{:T(128)}, bf16[512,2,4,128]{0,3,1,2:T(8,128)(2,1)}, bf16[512,2,4,128]{0,3,1,2:T(8,128)(2,1)}, f32[1536,4,128]{2,0,1:T(8,128)}, f32[1536,4,128...) while((s32[]{:T(128)}, ...), condition=%wide.region_4.5_spmd, body=%wide.region_0.4_spmd.sunk | while | flops 2434007552 | bytes 79718664 | solution.py:146
  108.9 6.1 %fusion.123 = (f32[2,512]{1,0:T(2,128)S(1)}, f32[2,512,1536]{1,2,0:T(8,128)}) fusion(pred[512,1536]{0,1:T(8,128)(4,1)S(1)} %get-tuple-element.393, bf16[1536,4,128]{2,0,1:T(8,128)(2,1)} %get-tuple-element.394, s32[]{:T(128)} %get-tuple-element.376, bf16[512,2,4,128]{3,0,1,2:T(8,128)(2,1)} %get-tuple-element.395), kind=kOutput, calls=%fused_computation.110.clone.1 | convolution fusion | flops 408946176 | bytes 7738368 | tf_op jit(solution)/shard_map/while/body/eval_jaxpr/sub | solution.py:79
  115.0 3.9 %fusion.124 = bf16[2,512,1536]{1,2,0:T(8,128)(2,1)S(1)} fusion(f32[2,512,1536]{1,2,0:T(8,128)} %get-tuple-element.361, f32[2,512]{1,0:T(2,128)S(1)} %get-tuple-element.362), kind=kLoop, calls=%fused_computation.14.clone.1 | loop fusion | flops 3145728 | bytes 9441280 | tf_op jit(solution)/shard_map/while/body/eval_jaxpr/convert_element_type | solution.py:81
  120.0 1.2 fusion.125
  121.2 2.9 fusion.127
  124.2 1.6 fusion.126
  125.8 1.9 fusion.128
  127.7 6.1 %fusion.123 = (f32[2,512]{1,0:T(2,128)S(1)}, f32[2,512,1536]{1,2,0:T(8,128)}) fusion(pred[512,1536]{0,1:T(8,128)(4,1)S(1)} %get-tuple-element.393, bf16[1536,4,128]{2,0,1:T(8,128)(2,1)} %get-tuple-element.394, s32[]{:T(128)} %get-tuple-element.376, bf16[512,2,4,128]{3,0,1,2:T(8,128)(2,1)} %get-tuple-element.395), kind=kOutput, calls=%fused_computation.110.clone.1 | convolution fusion | flops 408946176 | bytes 7738368 | tf_op jit(solution)/shard_map/while/body/eval_jaxpr/sub | solution.py:79
  133.8 3.9 %fusion.124 = bf16[2,512,1536]{1,2,0:T(8,128)(2,1)S(1)} fusion(f32[2,512,1536]{1,2,0:T(8,128)} %get-tuple-element.361, f32[2,512]{1,0:T(2,128)S(1)} %get-tuple-element.362), kind=kLoop, calls=%fused_computation.14.clone.1 | loop fusion | flops 3145728 | bytes 9441280 | tf_op jit(solution)/shard_map/while/body/eval_jaxpr/convert_element_type | solution.py:81
  138.8 1.2 fusion.125
  140.0 2.9 fusion.127
  142.9 1.6 fusion.126
  144.5 1.9 fusion.128
  146.4 6.1 %fusion.123 = (f32[2,512]{1,0:T(2,128)S(1)}, f32[2,512,1536]{1,2,0:T(8,128)}) fusion(pred[512,1536]{0,1:T(8,128)(4,1)S(1)} %get-tuple-element.393, bf16[1536,4,128]{2,0,1:T(8,128)(2,1)} %get-tuple-element.394, s32[]{:T(128)} %get-tuple-element.376, bf16[512,2,4,128]{3,0,1,2:T(8,128)(2,1)} %get-tuple-element.395), kind=kOutput, calls=%fused_computation.110.clone.1 | convolution fusion | flops 408946176 | bytes 7738368 | tf_op jit(solution)/shard_map/while/body/eval_jaxpr/sub | solution.py:79
  152.5 3.9 %fusion.124 = bf16[2,512,1536]{1,2,0:T(8,128)(2,1)S(1)} fusion(f32[2,512,1536]{1,2,0:T(8,128)} %get-tuple-element.361, f32[2,512]{1,0:T(2,128)S(1)} %get-tuple-element.362), kind=kLoop, calls=%fused_computation.14.clone.1 | loop fusion | flops 3145728 | bytes 9441280 | tf_op jit(solution)/shard_map/while/body/eval_jaxpr/convert_element_type | solution.py:81
  158.7 3.0 fusion.127
  161.6 1.6 fusion.126
  163.3 1.9 fusion.128
  165.1 6.1 %fusion.123 = (f32[2,512]{1,0:T(2,128)S(1)}, f32[2,512,1536]{1,2,0:T(8,128)}) fusion(pred[512,1536]{0,1:T(8,128)(4,1)S(1)} %get-tuple-element.393, bf16[1536,4,128]{2,0,1:T(8,128)(2,1)} %get-tuple-element.394, s32[]{:T(128)} %get-tuple-element.376, bf16[512,2,4,128]{3,0,1,2:T(8,128)(2,1)} %get-tuple-element.395), kind=kOutput, calls=%fused_computation.110.clone.1 | convolution fusion | flops 408946176 | bytes 7738368 | tf_op jit(solution)/shard_map/while/body/eval_jaxpr/sub | solution.py:79
  171.3 3.9 %fusion.124 = bf16[2,512,1536]{1,2,0:T(8,128)(2,1)S(1)} fusion(f32[2,512,1536]{1,2,0:T(8,128)} %get-tuple-element.361, f32[2,512]{1,0:T(2,128)S(1)} %get-tuple-element.362), kind=kLoop, calls=%fused_computation.14.clone.1 | loop fusion | flops 3145728 | bytes 9441280 | tf_op jit(solution)/shard_map/while/body/eval_jaxpr/convert_element_type | solution.py:81
  176.2 1.2 fusion.125
  177.4 2.9 fusion.127
  180.4 1.6 fusion.126
  182.0 1.9 fusion.128
  183.9 1.7 slice.44
  185.6 3.1 copy.247
  188.7 6.0 %all-to-all-start.6 = ((f32[2,16,32,4,128]{4,3,2,0,1:T(4,128)}), f32[2,16,32,4,128]{4,3,2,0,1:T(4,128)S(1)}, u32[]{:S(2)}, u32[]{:S(2)}) async-start(f32[2,16,32,4,128]{4,3,2,0,1:T(4,128)} %copy.247), calls=%async_computation.7 | async-start | bytes 4194304 | tf_op jit(solution)/shard_map/all_to_all | solution.py:43
  194.7 1.7 slice.42
  196.5 3.1 copy.242
  199.6 36.9 %all-to-all-done.6 = f32[2,16,32,4,128]{4,3,2,0,1:T(4,128)S(1)} async-done(((f32[2,16,32,4,128]{4,3,2,0,1:T(4,128)}), f32[2,16,32,4,128]{4,3,2,0,1:T(4,128)S(1)}, u32[]{:S(2)}, u32[]{:S(2)}) %all-to-all-start.6) | async-done | bytes 2097184 | tf_op jit(solution)/shard_map/all_to_all | solution.py:43
  236.5 1.4 copy-done
  237.9 9.8 %all-to-all-start.4 = ((f32[2,16,32,4,128]{4,3,2,0,1:T(4,128)}), f32[2,16,32,4,128]{4,3,2,0,1:T(4,128)S(1)}, u32[]{:S(2)}, u32[]{:S(2)}) async-start(f32[2,16,32,4,128]{4,3,2,0,1:T(4,128)} %copy.242), calls=%async_computation.4 | async-start | bytes 4194304 | tf_op jit(solution)/shard_map/all_to_all | solution.py:36
  247.6 3.9 %reshape.96 = f32[2,16,16384]{2,0,1:T(2,128)} reshape(f32[2,16,32,4,128]{4,3,2,0,1:T(4,128)} %copy-done) | data formatting | bytes 4194304 | tf_op jit(solution)/shard_map/reshape | solution.py:57
  251.5 4.2 %copy.300 = f32[2,16,16384]{2,1,0:T(8,128)} copy(f32[2,16,16384]{2,0,1:T(2,128)} %reshape.96) | data formatting | bytes 4194304 | tf_op jit(solution)/shard_map/reshape | solution.py:57
  255.7 3.6 dot_general.60
  259.3 3.5 fusion.59
  262.9 1.4 copy.250
  264.3 25.9 %all-to-all-done.4 = f32[2,16,32,4,128]{4,3,2,0,1:T(4,128)S(1)} async-done(((f32[2,16,32,4,128]{4,3,2,0,1:T(4,128)}), f32[2,16,32,4,128]{4,3,2,0,1:T(4,128)S(1)}, u32[]{:S(2)}, u32[]{:S(2)}) %all-to-all-start.4) | async-done | bytes 2097184 | tf_op jit(solution)/shard_map/all_to_all | solution.py:36
  290.2 9.8 %all-to-all-start.7 = ((f32[16,32,4,128]{3,2,1,0:T(4,128)}), f32[16,32,4,128]{3,2,1,0:T(4,128)S(1)}, u32[]{:S(2)}, u32[]{:S(2)}) async-start(f32[16,32,4,128]{3,2,1,0:T(4,128)} %copy.250), calls=%async_computation.8 | async-start | bytes 2097152 | tf_op jit(solution)/shard_map/all_to_all | solution.py:63
  300.0 2.7 reshape.95
  302.7 2.8 copy.301
  305.5 2.4 dot_general.57
  307.9 3.5 fusion.56
  311.4 1.4 copy.245
  312.8 10.8 %all-to-all-done.7 = f32[16,32,4,128]{3,2,1,0:T(4,128)S(1)} async-done(((f32[16,32,4,128]{3,2,1,0:T(4,128)}), f32[16,32,4,128]{3,2,1,0:T(4,128)S(1)}, u32[]{:S(2)}, u32[]{:S(2)}) %all-to-all-start.7) | async-done | bytes 1048608 | tf_op jit(solution)/shard_map/all_to_all | solution.py:63
  323.7 5.9 %all-to-all-start.5 = ((f32[16,32,4,128]{3,2,1,0:T(4,128)}), f32[16,32,4,128]{3,2,1,0:T(4,128)S(1)}, u32[]{:S(2)}, u32[]{:S(2)}) async-start(f32[16,32,4,128]{3,2,1,0:T(4,128)} %copy.245), calls=%async_computation.5 | async-start | bytes 2097152 | tf_op jit(solution)/shard_map/all_to_all | solution.py:62
  329.7 2.4 bitcast_add_fusion
  332.2 20.3 %all-to-all-done.5 = f32[16,32,4,128]{3,2,1,0:T(4,128)S(1)} async-done(((f32[16,32,4,128]{3,2,1,0:T(4,128)}), f32[16,32,4,128]{3,2,1,0:T(4,128)S(1)}, u32[]{:S(2)}, u32[]{:S(2)}) %all-to-all-start.5) | async-done | bytes 1048608 | tf_op jit(solution)/shard_map/all_to_all | solution.py:62
  352.6 2.4 bitcast_add_fusion.1
  355.1 1.5 copy.252
  356.6 1.5 copy.253
  360.1 3.9 %reduce-scatter.3.cloned.1.call-done = f32[512,2,128]{2,0,1:T(8,128)} async-done(((f32[512,4,128]{2,0,1:T(8,128)}), f32[512,2,128]{2,0,1:T(8,128)}) %reduce-scatter.3.cloned.1.call-update) | async-done | bytes 524304 | tf_op jit(solution)/shard_map/reduce_scatter | solution.py:149
  (131 shorter events, 29.2 us)
Async XLA Ops:
  7.2 23.4 %all-to-all-start = ((bf16[512,4,128]{2,1,0:T(4,128)(2,1)}), bf16[512,4,128]{2,1,0:T(4,128)(2,1)S(1)}, u32[]{:S(2)}, u32[]{:S(2)}) async-start(bf16[512,4,128]{2,1,0:T(4,128)(2,1)} %param.9), calls=%async_computation | async-start | bytes 1048576 | tf_op jit(solution)/shard_map/all_to_all | solution.py:10
  30.6 18.4 %all-to-all-start.2 = ((bf16[512,4,128]{2,1,0:T(4,128)(2,1)}), bf16[512,4,128]{2,1,0:T(4,128)(2,1)S(1)}, u32[]{:S(2)}, u32[]{:S(2)}) async-start(bf16[512,4,128]{2,1,0:T(4,128)(2,1)} %param.8), calls=%async_computation.2 | async-start | bytes 1048576 | tf_op jit(solution)/shard_map/all_to_all | solution.py:9
  49.0 27.5 %all-to-all-start.1 = ((bf16[16,2,1,32,4,128]{5,3,4,1,2,0:T(8,128)(2,1)}), bf16[16,2,1,32,4,128]{5,3,4,1,2,0:T(8,128)(2,1)S(1)}, u32[]{:S(2)}, u32[]{:S(2)}) async-start(bf16[16,2,1,32,4,128]{5,3,4,1,2,0:T(8,128)(2,1)} %fusion.62), calls=%async_computation.1 | async-start | bytes 2097152 | tf_op jit(solution)/shard_map/all_to_all | solution.py:20
  53.0 29.4 %copy-start.3 = (bf16[512,4,128]{2,1,0:T(4,128)(2,1)S(1)}, bf16[512,4,128]{2,1,0:T(4,128)(2,1)}, u32[]{:S(2)}) copy-start(bf16[512,4,128]{2,1,0:T(4,128)(2,1)} %param.9) | copy-start | bytes 1572868
  53.8 29.5 %copy-start.4 = (bf16[512,4,128]{2,1,0:T(4,128)(2,1)S(1)}, bf16[512,4,128]{2,1,0:T(4,128)(2,1)}, u32[]{:S(2)}) copy-start(bf16[512,4,128]{2,1,0:T(4,128)(2,1)} %param.8) | copy-start | bytes 1572868
  53.8 30.4 %copy-start.12 = (s32[16,2]{0,1:T(2,128)S(1)}, s32[16,2]{0,1:T(2,128)}, u32[]{:S(2)}) copy-start(s32[16,2]{0,1:T(2,128)} %param.11) | copy-start | bytes 388
  76.5 28.8 %all-to-all-start.3 = ((bf16[2,16,32,4,128]{4,2,3,0,1:T(8,128)(2,1)}), bf16[2,16,32,4,128]{4,2,3,0,1:T(8,128)(2,1)S(1)}, u32[]{:S(2)}, u32[]{:S(2)}) async-start(bf16[2,16,32,4,128]{4,2,3,0,1:T(8,128)(2,1)} %copy.235), calls=%async_computation.3 | async-start | bytes 2097152 | tf_op jit(solution)/shard_map/all_to_all | solution.py:18
  105.4 1.0 copy-start.1
  105.4 1.2 copy-start.2
  106.6 2.4 copy-start.11
  115.0 4.6 %slice-start = ((s8[6291456]{0:T(1024)(128)(4,1)}), s8[4194304]{0:T(1024)(128)(4,1)S(1)}, s32[]{:S(2)}) async-start(s8[6291456]{0:T(1024)(128)(4,1)} %bitcast.265), calls=%async_computation.12 | async-start | bytes 8388608 | tf_op jit(solution)/shard_map/while
  115.0 3.9 %copy-start.5 = (bf16[512,2,4,128]{0,3,1,2:T(8,128)(2,1)S(1)}, bf16[512,2,4,128]{0,3,1,2:T(8,128)(2,1)}, u32[]{:S(2)}) copy-start(bf16[512,2,4,128]{0,3,1,2:T(8,128)(2,1)} %get-tuple-element.377) | copy-start | bytes 3145732 | tf_op jit(solution)/shard_map/while
  115.0 5.0 %slice-start.1 = ((s8[6291456]{0:T(1024)(128)(4,1)}), s8[2097152]{0:T(1024)(128)(4,1)S(1)}, s32[]{:S(2)}) async-start(s8[6291456]{0:T(1024)(128)(4,1)} %bitcast.265), calls=%async_computation.13 | async-start | bytes 4194304 | tf_op jit(solution)/shard_map/while
  119.6 1.7 copy-start.6
  121.2 2.9 copy-start.8
  125.8 1.9 copy-start.9
  133.8 4.6 %slice-start = ((s8[6291456]{0:T(1024)(128)(4,1)}), s8[4194304]{0:T(1024)(128)(4,1)S(1)}, s32[]{:S(2)}) async-start(s8[6291456]{0:T(1024)(128)(4,1)} %bitcast.265), calls=%async_computation.12 | async-start | bytes 8388608 | tf_op jit(solution)/shard_map/while
  133.8 3.9 %copy-start.5 = (bf16[512,2,4,128]{0,3,1,2:T(8,128)(2,1)S(1)}, bf16[512,2,4,128]{0,3,1,2:T(8,128)(2,1)}, u32[]{:S(2)}) copy-start(bf16[512,2,4,128]{0,3,1,2:T(8,128)(2,1)} %get-tuple-element.377) | copy-start | bytes 3145732 | tf_op jit(solution)/shard_map/while
  133.8 5.0 %slice-start.1 = ((s8[6291456]{0:T(1024)(128)(4,1)}), s8[2097152]{0:T(1024)(128)(4,1)S(1)}, s32[]{:S(2)}) async-start(s8[6291456]{0:T(1024)(128)(4,1)} %bitcast.265), calls=%async_computation.13 | async-start | bytes 4194304 | tf_op jit(solution)/shard_map/while
  138.3 1.7 copy-start.6
  140.0 2.9 copy-start.8
  144.5 1.9 copy-start.9
  152.5 4.6 %slice-start = ((s8[6291456]{0:T(1024)(128)(4,1)}), s8[4194304]{0:T(1024)(128)(4,1)S(1)}, s32[]{:S(2)}) async-start(s8[6291456]{0:T(1024)(128)(4,1)} %bitcast.265), calls=%async_computation.12 | async-start | bytes 8388608 | tf_op jit(solution)/shard_map/while
  152.5 3.9 %copy-start.5 = (bf16[512,2,4,128]{0,3,1,2:T(8,128)(2,1)S(1)}, bf16[512,2,4,128]{0,3,1,2:T(8,128)(2,1)}, u32[]{:S(2)}) copy-start(bf16[512,2,4,128]{0,3,1,2:T(8,128)(2,1)} %get-tuple-element.377) | copy-start | bytes 3145732 | tf_op jit(solution)/shard_map/while
  152.5 5.0 %slice-start.1 = ((s8[6291456]{0:T(1024)(128)(4,1)}), s8[2097152]{0:T(1024)(128)(4,1)S(1)}, s32[]{:S(2)}) async-start(s8[6291456]{0:T(1024)(128)(4,1)} %bitcast.265), calls=%async_computation.13 | async-start | bytes 4194304 | tf_op jit(solution)/shard_map/while
  157.0 1.7 copy-start.6
  158.7 3.0 copy-start.8
  163.3 1.9 copy-start.9
  171.2 4.6 %slice-start = ((s8[6291456]{0:T(1024)(128)(4,1)}), s8[4194304]{0:T(1024)(128)(4,1)S(1)}, s32[]{:S(2)}) async-start(s8[6291456]{0:T(1024)(128)(4,1)} %bitcast.265), calls=%async_computation.12 | async-start | bytes 8388608 | tf_op jit(solution)/shard_map/while
  171.3 3.9 %copy-start.5 = (bf16[512,2,4,128]{0,3,1,2:T(8,128)(2,1)S(1)}, bf16[512,2,4,128]{0,3,1,2:T(8,128)(2,1)}, u32[]{:S(2)}) copy-start(bf16[512,2,4,128]{0,3,1,2:T(8,128)(2,1)} %get-tuple-element.377) | copy-start | bytes 3145732 | tf_op jit(solution)/shard_map/while
  171.3 5.0 %slice-start.1 = ((s8[6291456]{0:T(1024)(128)(4,1)}), s8[2097152]{0:T(1024)(128)(4,1)S(1)}, s32[]{:S(2)}) async-start(s8[6291456]{0:T(1024)(128)(4,1)} %bitcast.265), calls=%async_computation.13 | async-start | bytes 4194304 | tf_op jit(solution)/shard_map/while
  175.8 1.7 copy-start.6
  177.4 2.9 copy-start.8
  182.0 1.9 copy-start.9
  188.7 47.8 %all-to-all-start.6 = ((f32[2,16,32,4,128]{4,3,2,0,1:T(4,128)}), f32[2,16,32,4,128]{4,3,2,0,1:T(4,128)S(1)}, u32[]{:S(2)}, u32[]{:S(2)}) async-start(f32[2,16,32,4,128]{4,3,2,0,1:T(4,128)} %copy.247), calls=%async_computation.7 | async-start | bytes 4194304 | tf_op jit(solution)/shard_map/all_to_all | solution.py:43
  236.5 1.4 copy-start
  237.9 52.3 %all-to-all-start.4 = ((f32[2,16,32,4,128]{4,3,2,0,1:T(4,128)}), f32[2,16,32,4,128]{4,3,2,0,1:T(4,128)S(1)}, u32[]{:S(2)}, u32[]{:S(2)}) async-start(f32[2,16,32,4,128]{4,3,2,0,1:T(4,128)} %copy.242), calls=%async_computation.4 | async-start | bytes 4194304 | tf_op jit(solution)/shard_map/all_to_all | solution.py:36
  290.2 33.5 %all-to-all-start.7 = ((f32[16,32,4,128]{3,2,1,0:T(4,128)}), f32[16,32,4,128]{3,2,1,0:T(4,128)S(1)}, u32[]{:S(2)}, u32[]{:S(2)}) async-start(f32[16,32,4,128]{3,2,1,0:T(4,128)} %copy.250), calls=%async_computation.8 | async-start | bytes 2097152 | tf_op jit(solution)/shard_map/all_to_all | solution.py:63
  323.7 28.8 %all-to-all-start.5 = ((f32[16,32,4,128]{3,2,1,0:T(4,128)}), f32[16,32,4,128]{3,2,1,0:T(4,128)S(1)}, u32[]{:S(2)}, u32[]{:S(2)}) async-start(f32[16,32,4,128]{3,2,1,0:T(4,128)} %copy.245), calls=%async_computation.5 | async-start | bytes 2097152 | tf_op jit(solution)/shard_map/all_to_all | solution.py:62
  329.5 28.5 %reduce-scatter.5.cloned.1.call-start = ((), (), s32[]{:S(2)}) async-start(), calls=%async_computation.11 | async-start | bytes 1572864 | tf_op jit(solution)/shard_map/reduce_scatter | solution.py:150
  332.1 23.0 %copy-start.7 = (bf16[512,2,4,128]{0,3,1,2:T(8,128)(2,1)S(1)}, bf16[512,2,4,128]{0,3,1,2:T(8,128)(2,1)}, u32[]{:S(2)}) copy-start(bf16[512,2,4,128]{0,3,1,2:T(8,128)(2,1)} %get-tuple-element.260) | copy-start | bytes 3145732
  332.1 31.9 %reduce-scatter.3.cloned.1.call-start = ((), (), s32[]{:S(2)}) async-start(), calls=%async_computation.10 | async-start | bytes 1572864 | tf_op jit(solution)/shard_map/reduce_scatter | solution.py:149
  352.6 4.0 %copy-start.10 = (bf16[512,2,4,128]{0,3,1,2:T(8,128)(2,1)S(1)}, bf16[512,2,4,128]{0,3,1,2:T(8,128)(2,1)}, u32[]{:S(2)}) copy-start(bf16[512,2,4,128]{0,3,1,2:T(8,128)(2,1)} %get-tuple-element.261) | copy-start | bytes 3145732
Sparse Core Ops, SparseCore 0:
  332.6 9.6 reduce-scatter.4
  355.2 8.7 reduce-scatter.2
